TPU v7x, 512 devices: a whole 4x4x16 slice. The times are simulated.
512 devices in a mesh: blk: 64 (over y, z_hi, x, core), group: 8 (over z_lo).
Axes of the slice: x: 4, y: 4, z: 16 (z_hi: 2, z_lo: 8; z = z_hi * 8 + z_lo), core: 2. Of those that a mesh axis runs over, the one named last changes fastest.
Arguments:
- sketch: bfloat16 [32768, 768], P('blk'), may hold values from -6 to 6
- far_tiles: bfloat16 [64, 8, 3, 6, 128, 512], P('blk', 'group'), may hold values from -0.1875 to 0.1875
- row_blocks: int32 [64, 8, 3, 6], P('blk', 'group'), may hold values from 0 to 7, as said below
- owner_route: int32 [64, 8, 8], P('blk', 'group'), may hold values from 0 to 7, each once within a row
- cluster_basis: bfloat16 [64, 8, 1024, 256], P('blk', 'group'), may hold values from -0.1875 to 0.1875
Outputs:
- coefficients: float32 [64, 8, 256, 768], P('blk', 'group')
Inputs may be any that keep to these rules, and one draw needn't show every extreme that they name: `row_blocks`: for one device and one offset, the 6 entries are distinct. `owner_route`: for each device the entries are a permutation of 0 .. 8 - 1.
All inputs are finite; a program needn't handle non-finite values.
Results may differ from a plain program's by a relative error of at most 0.0029.
Values may be sent and summed in bfloat16 or wider, within the bound.
A program may use at most 64 MiB of HBM per device.

v0:
```python
import jax
import jax.numpy as jnp
from jax import lax
from jax.sharding import PartitionSpec as P


def from_behind(array, axis, by):
    devices = lax.axis_size(axis)
    return lax.ppermute(array, axis, [(i, (i + by) % devices) for i in range(devices)])


def contribute(summed, far_tiles, row_blocks, offset, current):
    product = jnp.einsum(
        "trk,kc->trc", far_tiles[0, 0, offset], current, preferred_element_type=jnp.float32
    )
    return summed.at[row_blocks[0, 0, offset]].add(product)


def body(sketch, far_tiles, row_blocks, owner_route, cluster_basis):
    offsets = far_tiles.shape[2]
    radius = (offsets - 1) // 2
    groups = lax.axis_size("group")
    tile_rows = far_tiles.shape[4]
    columns = sketch.shape[1]
    summed = jnp.zeros((groups, tile_rows, columns), jnp.float32)
    current = from_behind(sketch, "blk", -radius)
    summed = contribute(summed, far_tiles, row_blocks, 2 * radius, current)
    for hop_count in range(1, 2 * radius + 1):
        current = from_behind(current, "blk", 1)
        summed = contribute(summed, far_tiles, row_blocks, 2 * radius - hop_count, current)
    sampled = summed.astype(jnp.bfloat16)
    ordered = jnp.zeros_like(sampled).at[owner_route[0, 0]].set(sampled)
    basis_local = cluster_basis[0, 0]
    received = lax.all_to_all(ordered, "group", split_axis=0, concat_axis=0, tiled=True)
    stacked = received.reshape(received.shape[0] * received.shape[1], received.shape[2])
    coefficients = lax.dot_general(
        basis_local, stacked, (((0,), (0,)), ((), ())), preferred_element_type=jnp.float32
    )
    return coefficients[None, None]


def solution(mesh):
    placed = (
        P("blk", None),
        P("blk", "group", None, None, None, None),
        P("blk", "group", None, None),
        P("blk", "group", None),
        P("blk", "group", None, None),
    )
    return jax.shard_map(
        body, mesh=mesh, in_specs=placed, out_specs=P("blk", "group", None, None), check_vma=False
    )
```

profile of v0, /device:TPU:16, one launch (start us, length us, event | category | flops | bytes accessed | tf_op | source)
XLA Modules:
  0.0 215.7 jit_solution(8105737599736521911)
XLA Ops:
  0.0 0.0 copy-start
  0.0 17.4 %collective-permute-start = (bf16[512,768]{1,0:T(8,128)(2,1)}, bf16[512,768]{1,0:T(8,128)(2,1)S(1)}, u32[]{:S(2)}, u32[]{:S(2)}) collective-permute-start(bf16[512,768]{1,0:T(8,128)(2,1)} %param.5), channel_id=1, source_target_pairs={{0,504},{8,0},{16,8},{24,16},{32,24},{40,32},{48,40},{56,48},{64,5... | collective-permute-start | bytes 2359304 | tf_op jit(solution)/shard_map/ppermute | solution.py:9
  17.4 34.3 %collective-permute-done = bf16[512,768]{1,0:T(8,128)(2,1)S(1)} collective-permute-done((bf16[512,768]{1,0:T(8,128)(2,1)}, bf16[512,768]{1,0:T(8,128)(2,1)S(1)}, u32[]{:S(2)}, u32[]{:S(2)}) %collective-permute-start) | collective-permute-done | bytes 786464 | tf_op jit(solution)/shard_map/ppermute | solution.py:9
  51.7 1.9 collective-permute-start.1
  53.6 0.7 fusion.16
  54.3 35.5 %collective-permute-done.1 = bf16[512,768]{1,0:T(8,128)(2,1)} collective-permute-done((bf16[512,768]{1,0:T(8,128)(2,1)S(1)}, bf16[512,768]{1,0:T(8,128)(2,1)}, u32[]{:S(2)}, u32[]{:S(2)}) %collective-permute-start.1) | collective-permute-done | bytes 786464 | tf_op jit(solution)/shard_map/ppermute | solution.py:9
  89.7 1.9 collective-permute-start.2
  91.7 0.7 fusion.13
  92.3 1.9 fusion.6
  94.2 1.9 broadcast_in_dim.14
  96.2 6.6 %scatter_fusion = f32[8,128,768]{2,1,0:T(8,128)} fusion(f32[8,128,768]{2,1,0:T(8,128)} %broadcast_in_dim.14, s32[6]{0:T(128)S(1)} %get-tuple-element.6, f32[6,128,768]{2,1,0:T(8,128)S(1)} %fusion.6), kind=kCustom, calls=%fused_computation | custom fusion | flops 589824 | bytes 7077912 | tf_op jit(solution)/shard_map/scatter-add | solution.py:16
  102.8 2.1 fusion.3
  105.0 6.6 %scatter_fusion.1 = f32[8,128,768]{2,1,0:T(8,128)} fusion(f32[8,128,768]{2,1,0:T(8,128)} %scatter_fusion, s32[6]{0:T(128)S(1)} %get-tuple-element.7, f32[6,128,768]{2,1,0:T(8,128)S(1)} %fusion.3), kind=kCustom, calls=%fused_computation.1 | custom fusion | flops 589824 | bytes 7077912 | tf_op jit(solution)/shard_map/scatter-add | solution.py:16
  111.6 21.5 %collective-permute-done.2 = bf16[512,768]{1,0:T(8,128)(2,1)} collective-permute-done((bf16[512,768]{1,0:T(8,128)(2,1)}, bf16[512,768]{1,0:T(8,128)(2,1)}, u32[]{:S(2)}, u32[]{:S(2)}) %collective-permute-start.2) | collective-permute-done | bytes 786464 | tf_op jit(solution)/shard_map/ppermute | solution.py:9
  133.1 2.1 fusion
  135.2 6.6 %scatter_fusion.2 = f32[8,128,768]{2,1,0:T(8,128)} fusion(f32[8,128,768]{2,1,0:T(8,128)} %scatter_fusion.1, s32[6]{0:T(128)S(1)} %get-tuple-element.5, f32[6,128,768]{2,1,0:T(8,128)S(1)} %fusion), kind=kCustom, calls=%fused_computation.2 | custom fusion | flops 589824 | bytes 7077912 | tf_op jit(solution)/shard_map/scatter-add | solution.py:16
  141.8 3.2 %convert_element_type.3 = bf16[8,128,768]{2,1,0:T(8,128)(2,1)} convert(f32[8,128,768]{2,1,0:T(8,128)} %scatter_fusion.2) | non-fusion elementwise | flops 786432 | bytes 4718592 | tf_op jit(solution)/shard_map/convert_element_type | solution.py:31
  145.0 0.1 broadcast_in_dim.6
  145.1 3.1 %scatter_fusion.3 = bf16[8,128,768]{2,1,0:T(8,128)(2,1)S(1)} fusion(bf16[8,128,768]{2,1,0:T(8,128)(2,1)S(1)} %broadcast_in_dim.6, s32[8]{0:T(128)S(1)} %fusion.13, bf16[8,128,768]{2,1,0:T(8,128)(2,1)} %convert_element_type.3), kind=kCustom, calls=%fused_computation.3 | custom fusion | bytes 4718624 | tf_op jit(solution)/shard_map/scatter | solution.py:32
  148.2 65.7 %all_to_all.5 = bf16[8,128,768]{2,1,0:T(8,128)(2,1)S(1)} all-to-all(bf16[8,128,768]{2,1,0:T(8,128)(2,1)S(1)} %scatter_fusion.3), channel_id=1, replica_groups=mesh['blk'=64,'group'=8] {'group'}, dimensions={0} | all-to-all | bytes 3145728 | tf_op jit(solution)/shard_map/all_to_all | solution.py:34
  213.9 0.0 copy-done
  213.9 0.6 convolution_bitcast_fusion
  214.5 1.1 copy.6
Async XLA Ops:
  0.0 213.9 %copy-start = (bf16[1,1,1024,256]{3,2,1,0:T(8,128)(2,1)S(1)}, bf16[1,1,1024,256]{3,2,1,0:T(8,128)(2,1)}, u32[]{:S(2)}) copy-start(bf16[1,1,1024,256]{3,2,1,0:T(8,128)(2,1)} %param.9) | copy-start | bytes 1572868
  0.0 51.7 %collective-permute-start = (bf16[512,768]{1,0:T(8,128)(2,1)}, bf16[512,768]{1,0:T(8,128)(2,1)S(1)}, u32[]{:S(2)}, u32[]{:S(2)}) collective-permute-start(bf16[512,768]{1,0:T(8,128)(2,1)} %param.5), channel_id=1, source_target_pairs={{0,504},{8,0},{16,8},{24,16},{32,24},{40,32},{48,40},{56,48},{64,5... | collective-permute-start | bytes 2359304 | tf_op jit(solution)/shard_map/ppermute | solution.py:9
  51.7 38.1 %collective-permute-start.1 = (bf16[512,768]{1,0:T(8,128)(2,1)S(1)}, bf16[512,768]{1,0:T(8,128)(2,1)}, u32[]{:S(2)}, u32[]{:S(2)}) collective-permute-start(bf16[512,768]{1,0:T(8,128)(2,1)S(1)} %collective-permute-done), channel_id=1, source_target_pairs={{0,8},{8,16},{16,24},{24,32},{32,40},{40,48},{48,56},{56,64},{64,7... | collective-permute-start | bytes 2359304 | tf_op jit(solution)/shard_map/ppermute | solution.py:9
  89.7 43.4 %collective-permute-start.2 = (bf16[512,768]{1,0:T(8,128)(2,1)}, bf16[512,768]{1,0:T(8,128)(2,1)}, u32[]{:S(2)}, u32[]{:S(2)}) collective-permute-start(bf16[512,768]{1,0:T(8,128)(2,1)} %collective-permute-done.1), channel_id=1, source_target_pairs={{0,8},{8,16},{16,24},{24,32},{32,40},{40,48},{48,56},{56,64},{64,7... | collective-permute-start | bytes 2359304 | tf_op jit(solution)/shard_map/ppermute | solution.py:9
where the time goes:
time: 217 us; the launch traced here: 216 us
  waiting for transfers between devices  91.3 us (42%)
  blocking collectives  65.7 us (30%)
  other arithmetic  24.4 us (11%)
  starting transfers between devices  21.2 us (10%)
  matrix products  6.79 us (3%)
  local copies, waits for them, and re-layouts  6.28 us (3%)
    ppermute x3, waiting for transfers between devices, from_behind(): lax.ppermute(array, axis, [(i, (i + by) % devices) for i in range(devices)])  91.3 us
    all_to_all x1, blocking collectives, body(): lax.all_to_all(ordered, 'group', split_axis=0, concat_axis=0, tiled=True)  65.7 us
    ppermute x3, starting transfers between devices, from_behind(): lax.ppermute(array, axis, [(i, (i + by) % devices) for i in range(devices)])  21.2 us
    scatter-add x3, other arithmetic, contribute(): return summed.at[row_blocks[0, 0, offset]].add(product)  19.9 us
    dot_general x3, matrix products, contribute(): jnp.einsum('trk,kc->trc', far_tiles[0, 0, offset], current, preferred_ele...  6.19 us
  transfers between devices with their start and end apart: 3, of which 3 were waited for; matrix products, arithmetic and copies ran while one was open for 10% of the time, Pallas kernels for 0%

commit v1 on v0

v1 whole, which is shorter than its diff:
```python
import functools

import jax
import jax.numpy as jnp
from jax import lax
from jax.experimental import pallas as pl
from jax.experimental.pallas import tpu as pltpu
from jax.sharding import PartitionSpec as P

MESH = pl.DeviceIdType.MESH
ROW = 8
WIDTH = 128
BAND = 256


def kernel(
    blks, groups,
    sketch, far_tiles, row_blocks, owner_route, cluster_basis, out,
    window, tiles, lefts, ordered, received, basis, basis_t,
    in_sem, halo_send, halo_recv, relay_send, block_send, block_recv,
):
    b = lax.axis_index("blk")
    g = lax.axis_index("group")
    offsets, slots, tile_rows, panels = far_tiles.shape[2:]
    chunks = window.shape[0]
    half = groups // 2
    low, high = lax.rem(b, ROW) == 0, lax.rem(b, ROW) == ROW - 1
    end = (g == 0) | (g == groups - 1)
    before = (lax.rem(b + blks - 1, blks), jnp.where(low, groups - 1 - g, g))
    after = (lax.rem(b + 1, blks), jnp.where(high, groups - 1 - g, g))
    sends_before = jnp.logical_not(low) | end
    sends_after = jnp.logical_not(high) | end
    inward = (b, jnp.where(g < half, g + 1, g - 1))
    passes_on = (g != half - 1) & (g != half)

    def own_chunk(k):
        return pltpu.make_async_copy(
            sketch.at[:, pl.ds(k * WIDTH, WIDTH)], window.at[k, 1], in_sem.at[k]
        )

    tiles_in = pltpu.make_async_copy(
        far_tiles.at[0, 0], tiles.at[:, pl.ds(0, slots)], in_sem.at[chunks]
    )
    basis_in = pltpu.make_async_copy(cluster_basis.at[0, 0], basis, in_sem.at[chunks + 1])

    def to_before(k):
        return pltpu.make_async_remote_copy(
            src_ref=window.at[k, 1], dst_ref=window.at[k, 2],
            send_sem=halo_send.at[0, k], recv_sem=halo_recv.at[1, k],
            device_id=before, device_id_type=MESH,
        )

    def to_after(k):
        return pltpu.make_async_remote_copy(
            src_ref=window.at[k, 1], dst_ref=window.at[k, 0],
            send_sem=halo_send.at[1, k], recv_sem=halo_recv.at[0, k],
            device_id=after, device_id_type=MESH,
        )

    def relay(k, place):
        return pltpu.make_async_remote_copy(
            src_ref=window.at[k, place], dst_ref=window.at[k, place],
            send_sem=relay_send.at[k], recv_sem=halo_recv.at[place // 2, k],
            device_id=inward, device_id_type=MESH,
        )

    def block(k, owner):
        return pltpu.make_async_remote_copy(
            src_ref=ordered.at[k, owner], dst_ref=received.at[k, g],
            send_sem=block_send.at[k, owner], recv_sem=block_recv.at[k, g],
            device_id=(b, owner), device_id_type=MESH,
        )

    def from_peer(k, peer):
        return pltpu.make_async_remote_copy(
            src_ref=ordered.at[k, peer], dst_ref=received.at[k, peer],
            send_sem=block_send.at[k, peer], recv_sem=block_recv.at[k, peer],
            device_id=(b, peer), device_id_type=MESH,
        )

    barrier = pltpu.get_barrier_semaphore()
    for step in range(1, groups):
        pl.semaphore_signal(
            barrier, inc=1, device_id=(b, lax.rem(g + step, groups)), device_id_type=MESH
        )

    @pl.when(sends_before)
    def _():
        pl.semaphore_signal(barrier, inc=1, device_id=before, device_id_type=MESH)

    @pl.when(sends_after)
    def _():
        pl.semaphore_signal(barrier, inc=1, device_id=after, device_id_type=MESH)

    for k in range(chunks):
        own_chunk(k).start()
    tiles_in.start()
    basis_in.start()
    tiles[:, slots] = jnp.zeros((offsets, tile_rows, panels), tiles.dtype)

    pl.semaphore_wait(
        barrier, groups - 1 + sends_before.astype(jnp.int32) + sends_after.astype(jnp.int32)
    )

    for k in range(chunks):
        own_chunk(k).wait()

        @pl.when(sends_before)
        def _():
            to_before(k).start()

        @pl.when(sends_after)
        def _():
            to_after(k).start()

    tiles_in.wait()
    for offset in range(offsets):
        owners = [owner_route[row_blocks[offset, slot]] for slot in range(slots)]
        for owner in range(groups):
            slot = jnp.int32(slots)
            for candidate in range(slots):
                slot = jnp.where(owners[candidate] == owner, candidate, slot)
            lefts[
                pl.ds(owner * tile_rows, tile_rows), pl.ds(offset * panels, panels)
            ] = tiles[offset, slot]

    per_band = BAND // tile_rows
    bands = groups // per_band

    def sample(k, _):
        pltpu.make_async_remote_copy(
            src_ref=window.at[k, 1], dst_ref=window.at[k, 0],
            send_sem=halo_send.at[1, k], recv_sem=halo_recv.at[0, k],
            device_id=after, device_id_type=MESH,
        ).wait_recv()

        @pl.when(low & passes_on)
        def _():
            relay(k, 0).start()

        pltpu.make_async_remote_copy(
            src_ref=window.at[k, 1], dst_ref=window.at[k, 2],
            send_sem=halo_send.at[0, k], recv_sem=halo_recv.at[1, k],
            device_id=before, device_id_type=MESH,
        ).wait_recv()

        @pl.when(high & passes_on)
        def _():
            relay(k, 2).start()

        panels_in = window[k].reshape(offsets * panels, WIDTH)

        def band(step, _):
            place = lax.rem(step + jnp.where(g < half, bands // 2, 0), bands)
            rows = jnp.dot(
                lefts[pl.ds(pl.multiple_of(place * BAND, BAND), BAND), :],
                panels_in,
                preferred_element_type=jnp.float32,
            ).astype(jnp.bfloat16)
            for part in range(per_band):
                owner = place * per_band + part
                ordered[k, owner] = rows[part * tile_rows : (part + 1) * tile_rows]

                @pl.when(owner != g)
                def _():
                    block(k, owner).start()

            return 0

        lax.fori_loop(0, bands, band, 0)
        received[k, g] = ordered[k, g]
        return 0

    lax.fori_loop(0, chunks, sample, 0)

    basis_in.wait()
    basis_t[...] = basis[...].T

    for k in range(chunks):

        def arrive(step, _):
            from_peer(k, lax.rem(g + step, groups)).wait_recv()
            return 0

        lax.fori_loop(1, groups, arrive, 0)
        out[:, k * WIDTH : (k + 1) * WIDTH] = jnp.dot(
            basis_t[...],
            received[k].reshape(groups * tile_rows, WIDTH),
            preferred_element_type=jnp.float32,
        )

    def drain(k, _):
        def left(step, _):
            block(k, lax.rem(g + step, groups)).wait_send()
            return 0

        lax.fori_loop(1, groups, left, 0)

        @pl.when(sends_before)
        def _():
            to_before(k).wait_send()

        @pl.when(sends_after)
        def _():
            to_after(k).wait_send()

        @pl.when(low & passes_on)
        def _():
            relay(k, 0).wait_send()

        @pl.when(high & passes_on)
        def _():
            relay(k, 2).wait_send()

        return 0

    lax.fori_loop(0, chunks, drain, 0)


def solution(mesh):
    blks, groups = mesh.shape["blk"], mesh.shape["group"]

    def body(sketch, far_tiles, row_blocks, owner_route, cluster_basis):
        offsets, slots, tile_rows, panels = far_tiles.shape[2:]
        columns = sketch.shape[1]
        cluster_rows, rank = cluster_basis.shape[2:]
        chunks = columns // WIDTH
        kept = jnp.bfloat16
        coefficients = pl.pallas_call(
            functools.partial(kernel, blks, groups),
            out_shape=jax.ShapeDtypeStruct((rank, columns), jnp.float32),
            in_specs=[
                pl.BlockSpec(memory_space=pl.ANY),
                pl.BlockSpec(memory_space=pl.ANY),
                pl.BlockSpec(memory_space=pltpu.SMEM),
                pl.BlockSpec(memory_space=pltpu.SMEM),
                pl.BlockSpec(memory_space=pl.ANY),
            ],
            out_specs=pl.BlockSpec(memory_space=pltpu.VMEM),
            scratch_shapes=[
                pltpu.VMEM((chunks, offsets, panels, WIDTH), kept),
                pltpu.VMEM((offsets, slots + 1, tile_rows, panels), kept),
                pltpu.VMEM((groups * tile_rows, offsets * panels), kept),
                pltpu.VMEM((chunks, groups, tile_rows, WIDTH), kept),
                pltpu.VMEM((chunks, groups, tile_rows, WIDTH), kept),
                pltpu.VMEM((cluster_rows, rank), kept),
                pltpu.VMEM((rank, cluster_rows), kept),
                pltpu.SemaphoreType.DMA((chunks + 2,)),
                pltpu.SemaphoreType.DMA((2, chunks)),
                pltpu.SemaphoreType.DMA((2, chunks)),
                pltpu.SemaphoreType.DMA((chunks,)),
                pltpu.SemaphoreType.DMA((chunks, groups)),
                pltpu.SemaphoreType.DMA((chunks, groups)),
            ],
            compiler_params=pltpu.CompilerParams(
                collective_id=0, has_side_effects=True, vmem_limit_bytes=60 * 1024 * 1024
            ),
        )(sketch, far_tiles, row_blocks[0, 0], owner_route[0, 0], cluster_basis)
        return coefficients[None, None]

    placed = (
        P("blk", None),
        P("blk", "group", None, None, None, None),
        P("blk", "group", None, None),
        P("blk", "group", None),
        P("blk", "group", None, None),
    )
    return jax.shard_map(
        body, mesh=mesh, in_specs=placed, out_specs=P("blk", "group", None, None), check_vma=False
    )
```

time: 217 us -> 99.7 us (0.46)
  the two profiles are of different devices: /device:TPU:16 before, /device:TPU:8 now
where the time goes in v1:
time: 99.7 us; the launch traced here: 99.5 us
  Pallas kernels  96.1 us (96%)
  local copies, waits for them, and re-layouts  3.32 us (3%)
    pallas_call x1, Pallas kernels, body(): pl.pallas_call(functools.partial(kernel, blks, groups), out_shape=jax.Sha...  96.1 us
    unnamed x2, local copies, waits for them, and re-layouts  3.32 us

profile of v1, /device:TPU:8, one launch (start us, length us, event | category | flops | bytes accessed | tf_op | source)
XLA Modules:
  0.0 99.5 jit_solution(8091100014339823099)
XLA Ops:
  0.0 1.3 %copy.8 = s32[1,1,3,6]{3,2,1,0:T(4,128)} copy(s32[1,1,3,6]{3,1,2,0:T(1,128)} %param.7) | data formatting | bytes 144
  1.3 96.1 %shard_map.55 = f32[256,768]{1,0:T(8,128)} custom-call(bf16[512,768]{1,0:T(8,128)(2,1)} %sketch.1, bf16[1,1,3,6,128,512]{5,4,3,2,1,0:T(8,128)(2,1)} %far_tiles.1, s32[3,6]{1,0:T(4,128)} %bitcast.6, s32[8]{0:T(128)} %bitcast.7, bf16[1,1,1024,256]{3,2,1,0:T(8,128)(2,1)} %cluster_basis.1), custom_call_target="tpu_custom_call" | custom-call | tf_op jit(solution)/shard_map/pallas_call | solution.py:229
  97.4 2.1 %copy.10 = f32[1,1,256,768]{3,2,1,0:T(8,128)} copy(f32[1,1,256,768]{3,2,1,0:T(8,128)} %bitcast.5) | data formatting | bytes 1572864

commit v2 on v1

v2 whole, which is shorter than its diff:
```python
import functools

import jax
import jax.numpy as jnp
from jax import lax
from jax.experimental import pallas as pl
from jax.experimental.pallas import tpu as pltpu
from jax.sharding import PartitionSpec as P

MESH = pl.DeviceIdType.MESH
ROW = 8
WIDTH = 128
BAND = 256
PARTS = (1, 2, 3)


def kernel(
    blks, groups,
    sketch, far_tiles, row_blocks, owner_route, cluster_basis, out,
    window, tiles, lefts, ordered, received, basis, basis_t,
    in_sem, halo_send, halo_recv, edge_send,
    block_send, block_recv,
):
    b = lax.axis_index("blk")
    g = lax.axis_index("group")
    offsets, slots, tile_rows, panels = far_tiles.shape[2:]
    chunks = window.shape[0]
    half = groups // 2
    core = lax.rem(b, 2)
    low, high = lax.rem(b, ROW) == 0, lax.rem(b, ROW) == ROW - 1
    edge = low | high
    end = (g == 0) | (g == groups - 1)
    source = edge & end
    before, after = lax.rem(b + blks - 1, blks), lax.rem(b + 1, blks)
    def own_chunk(k):
        return pltpu.make_async_copy(
            sketch.at[:, pl.ds(k * WIDTH, WIDTH)], window.at[k, 1], in_sem.at[k]
        )

    tiles_in = pltpu.make_async_copy(
        far_tiles.at[0, 0], tiles.at[:, pl.ds(0, slots)], in_sem.at[chunks]
    )
    basis_in = pltpu.make_async_copy(cluster_basis.at[0, 0], basis, in_sem.at[chunks + 1])

    def to_before(k):
        return pltpu.make_async_remote_copy(
            src_ref=window.at[k, 1], dst_ref=window.at[k, 2],
            send_sem=halo_send.at[0, k], recv_sem=halo_recv.at[1, k],
            device_id=(before, g), device_id_type=MESH,
        )

    def to_after(k):
        return pltpu.make_async_remote_copy(
            src_ref=window.at[k, 1], dst_ref=window.at[k, 0],
            send_sem=halo_send.at[1, k], recv_sem=halo_recv.at[0, k],
            device_id=(after, g), device_id_type=MESH,
        )

    def across(k, group):
        return pltpu.make_async_remote_copy(
            src_ref=window.at[k, 1], dst_ref=window.at[k, 2 * (1 - core)],
            send_sem=edge_send.at[k, group % half], recv_sem=halo_recv.at[1 - core, k],
            device_id=(jnp.where(low, before, after), jnp.where(g == 0, group, group - half)),
            device_id_type=MESH,
        )

    starts = [sum(PARTS[:p]) for p in range(len(PARTS))]

    def block(p, owner):
        span = pl.ds(starts[p], PARTS[p])
        return pltpu.make_async_remote_copy(
            src_ref=ordered.at[span, owner], dst_ref=received.at[span, g],
            send_sem=block_send.at[p, owner], recv_sem=block_recv.at[p, g],
            device_id=(b, owner), device_id_type=MESH,
        )

    def from_peer(p, peer):
        span = pl.ds(starts[p], PARTS[p])
        return pltpu.make_async_remote_copy(
            src_ref=ordered.at[span, peer], dst_ref=received.at[span, peer],
            send_sem=block_send.at[p, peer], recv_sem=block_recv.at[p, peer],
            device_id=(b, peer), device_id_type=MESH,
        )

    barrier = pltpu.get_barrier_semaphore()

    def greet(blk, group):
        pl.semaphore_signal(barrier, inc=1, device_id=(blk, group), device_id_type=MESH)

    for step in range(1, groups):
        greet(b, lax.rem(g + step, groups))

    @pl.when(jnp.logical_not(low))
    def _():
        greet(before, g)

    @pl.when(jnp.logical_not(high))
    def _():
        greet(after, g)

    @pl.when(edge)
    def _():
        greet(jnp.where(low, before, after), jnp.where(g < half, groups - 1, 0))

    for k in range(chunks):
        own_chunk(k).start()
    tiles_in.start()
    basis_in.start()
    tiles[:, slots] = jnp.zeros((offsets, tile_rows, panels), tiles.dtype)

    pl.semaphore_wait(
        barrier, groups - 1 + jnp.where(edge, 1, 2) + jnp.where(source, half, 0)
    )

    for k in range(chunks):
        own_chunk(k).wait()

        @pl.when(source)
        def _():
            for group in range(half, groups):
                across(k, group).start()

        @pl.when(jnp.logical_not(low))
        def _():
            to_before(k).start()

        @pl.when(jnp.logical_not(high))
        def _():
            to_after(k).start()

    tiles_in.wait()
    for offset in range(offsets):
        owners = [owner_route[0, 0, row_blocks[0, offset, 0, slot]] for slot in range(slots)]
        for owner in range(groups):
            slot = jnp.int32(slots)
            for candidate in range(slots):
                slot = jnp.where(owners[candidate] == owner, candidate, slot)
            lefts[
                pl.ds(owner * tile_rows, tile_rows), pl.ds(offset * panels, panels)
            ] = tiles[offset, slot]

    per_band = BAND // tile_rows
    bands = groups // per_band

    def sample(k, sent):
        to_after(k).wait_recv()
        to_before(k).wait_recv()
        panels_in = window[k].reshape(offsets * panels, WIDTH)

        def band(step, _):
            at = lax.rem(step + jnp.where(g < half, bands // 2, 0), bands)
            rows = jnp.dot(
                lefts[pl.ds(pl.multiple_of(at * BAND, BAND), BAND), :],
                panels_in,
                preferred_element_type=jnp.float32,
            ).astype(jnp.bfloat16)
            for part in range(per_band):
                owner = at * per_band + part
                ordered[k, owner] = rows[part * tile_rows : (part + 1) * tile_rows]
                if sent is not None:

                    @pl.when(owner != g)
                    def _():
                        block(sent, owner).start()

            return 0

        lax.fori_loop(0, bands, band, 0)
        received[k, g] = ordered[k, g]

        return 0

    for p, count in enumerate(PARTS):
        if count == 1:
            sample(starts[p], p)
            continue
        lax.fori_loop(starts[p], starts[p] + count, lambda k, _: sample(k, None), 0)

        def send(step, _):
            block(p, lax.rem(g + step, groups)).start()
            return 0

        lax.fori_loop(1, groups, send, 0)

    basis_in.wait()
    basis_t[...] = basis[...].T
    out[...] = jnp.zeros_like(out)

    def gather(step, _):
        near = step < half
        peer = jnp.where(g < half, 0, half) + lax.rem(g + step, half)
        peer = jnp.where(near, peer, lax.rem(peer + half, groups))

        @pl.when(step > 0)
        def _():
            for p in range(len(PARTS)):
                from_peer(p, peer).wait_recv()

        part = basis_t[:, pl.ds(pl.multiple_of(peer * tile_rows, tile_rows), tile_rows)]
        for k in range(chunks):
            out[:, k * WIDTH : (k + 1) * WIDTH] += jnp.dot(
                part, received[k, peer], preferred_element_type=jnp.float32
            )
        return 0

    lax.fori_loop(0, groups, gather, 0)

    def drain_block(step, _):
        for p in range(len(PARTS)):
            block(p, lax.rem(g + step, groups)).wait_send()
        return 0

    lax.fori_loop(1, groups, drain_block, 0)

    def drain(k, _):
        @pl.when(source)
        def _():
            for group in range(half, groups):
                across(k, group).wait_send()

        @pl.when(jnp.logical_not(low))
        def _():
            to_before(k).wait_send()

        @pl.when(jnp.logical_not(high))
        def _():
            to_after(k).wait_send()

        return 0

    lax.fori_loop(0, chunks, drain, 0)


def solution(mesh):
    blks, groups = mesh.shape["blk"], mesh.shape["group"]

    def body(sketch, far_tiles, row_blocks, owner_route, cluster_basis):
        offsets, slots, tile_rows, panels = far_tiles.shape[2:]
        columns = sketch.shape[1]
        cluster_rows, rank = cluster_basis.shape[2:]
        chunks = columns // WIDTH
        kept = jnp.bfloat16
        coefficients = pl.pallas_call(
            functools.partial(kernel, blks, groups),
            out_shape=jax.ShapeDtypeStruct((rank, columns), jnp.float32),
            in_specs=[
                pl.BlockSpec(memory_space=pl.ANY),
                pl.BlockSpec(memory_space=pl.ANY),
                pl.BlockSpec(memory_space=pltpu.SMEM),
                pl.BlockSpec(memory_space=pltpu.SMEM),
                pl.BlockSpec(memory_space=pl.ANY),
            ],
            out_specs=pl.BlockSpec(memory_space=pltpu.VMEM),
            scratch_shapes=[
                pltpu.VMEM((chunks, offsets, panels, WIDTH), kept),
                pltpu.VMEM((offsets, slots + 1, tile_rows, panels), kept),
                pltpu.VMEM((groups * tile_rows, offsets * panels), kept),
                pltpu.VMEM((chunks, groups, tile_rows, WIDTH), kept),
                pltpu.VMEM((chunks, groups, tile_rows, WIDTH), kept),
                pltpu.VMEM((cluster_rows, rank), kept),
                pltpu.VMEM((rank, cluster_rows), kept),
                pltpu.SemaphoreType.DMA((chunks + 2,)),
                pltpu.SemaphoreType.DMA((2, chunks)),
                pltpu.SemaphoreType.DMA((2, chunks)),
                pltpu.SemaphoreType.DMA((chunks, groups // 2)),
                pltpu.SemaphoreType.DMA((len(PARTS), groups)),
                pltpu.SemaphoreType.DMA((len(PARTS), groups)),
            ],
            compiler_params=pltpu.CompilerParams(
                collective_id=0, has_side_effects=True, vmem_limit_bytes=60 * 1024 * 1024
            ),
        )(sketch, far_tiles, jnp.transpose(row_blocks, (0, 2, 1, 3)), owner_route, cluster_basis)
        return coefficients[None, None]

    placed = (
        P("blk", None),
        P("blk", "group", None, None, None, None),
        P("blk", "group", None, None),
        P("blk", "group", None),
        P("blk", "group", None, None),
    )
    return jax.shard_map(
        body, mesh=mesh, in_specs=placed, out_specs=P("blk", "group", None, None), check_vma=False
    )
```

time: 99.7 us -> 91.4 us (0.917)
  the two profiles are of different devices: /device:TPU:8 before, /device:TPU:504 now
where the time goes in v2:
time: 91.4 us; the launch traced here: 90.3 us
  Pallas kernels  88.2 us (96%)
  local copies, waits for them, and re-layouts  2.06 us (2%)
    pallas_call x1, Pallas kernels, body(): pl.pallas_call(functools.partial(kernel, blks, groups), out_shape=jax.Sha...  88.2 us
    unnamed x1, local copies, waits for them, and re-layouts  2.06 us

profile of v2, /device:TPU:504, one launch (start us, length us, event | category | flops | bytes accessed | tf_op | source)
XLA Modules:
  0.0 90.3 jit_solution(13341505985606304949)
XLA Ops:
  0.0 88.2 %shard_map.55 = f32[256,768]{1,0:T(8,128)} custom-call(bf16[512,768]{1,0:T(8,128)(2,1)} %sketch.1, bf16[1,1,3,6,128,512]{5,4,3,2,1,0:T(8,128)(2,1)} %far_tiles.1, s32[1,3,1,6]{3,2,1,0:T(1,128)} %bitcast.3, s32[1,1,8]{2,1,0:T(1,128)} %owner_route.1, bf16[1,1,1024,256]{3,2,1,0:T(8,128)(2,1)} %cluster_basis.1), custom_call_target="tpu_custom_call" | custom-call | tf_op jit(solution)/shard_map/pallas_call | solution.py:243
  88.2 2.1 %copy.7 = f32[1,1,256,768]{3,2,1,0:T(8,128)} copy(f32[1,1,256,768]{3,2,1,0:T(8,128)} %bitcast.2) | data formatting | bytes 1572864

commit v3 on v2

--- a/solution.py
+++ b/solution.py
@@ -8,7 +8,8 @@
 from jax.sharding import PartitionSpec as P
 
 MESH = pl.DeviceIdType.MESH
-ROW = 8
+LANES = 4
+ROW = 2 * LANES
 WIDTH = 128
 BAND = 256
 PARTS = (1, 2, 3)
@@ -18,7 +19,7 @@
     blks, groups,
     sketch, far_tiles, row_blocks, owner_route, cluster_basis, out,
     window, tiles, lefts, ordered, received, basis, basis_t,
-    in_sem, halo_send, halo_recv, edge_send,
+    in_sem, halo_send, halo_recv, piece_send, piece_recv, across_send, across_recv,
     block_send, block_recv,
 ):
     b = lax.axis_index("blk")
@@ -30,8 +31,17 @@
     low, high = lax.rem(b, ROW) == 0, lax.rem(b, ROW) == ROW - 1
     edge = low | high
     end = (g == 0) | (g == groups - 1)
-    source = edge & end
     before, after = lax.rem(b + blks - 1, blks), lax.rem(b + 1, blks)
+    piece = panels // LANES
+    row = b // ROW * ROW
+    lane = lax.rem(b, ROW) // 2
+    held = jnp.where(edge, 1, offsets)
+    splits, forwards = edge & end, end & jnp.logical_not(edge)
+    goal = jnp.where(core == 0, lax.rem(row + blks - 1, blks), lax.rem(row + ROW, blks))
+    feeders = jnp.where(low, lax.rem(row + blks - ROW, blks), lax.rem(row + ROW, blks)) + 1 - core
+
+    starts = [sum(PARTS[:p]) for p in range(len(PARTS))]
+
     def own_chunk(k):
         return pltpu.make_async_copy(
             sketch.at[:, pl.ds(k * WIDTH, WIDTH)], window.at[k, 1], in_sem.at[k]
@@ -56,15 +66,32 @@
             device_id=(after, g), device_id_type=MESH,
         )
 
-    def across(k, group):
-        return pltpu.make_async_remote_copy(
-            src_ref=window.at[k, 1], dst_ref=window.at[k, 2 * (1 - core)],
-            send_sem=edge_send.at[k, group % half], recv_sem=halo_recv.at[1 - core, k],
-            device_id=(jnp.where(low, before, after), jnp.where(g == 0, group, group - half)),
-            device_id_type=MESH,
-        )
-
-    starts = [sum(PARTS[:p]) for p in range(len(PARTS))]
+    def spread(p, step):
+        lane_to = lax.rem(lane + step, LANES)
+        rows = pl.ds(pl.multiple_of(lane_to * piece, piece), piece)
+        span = pl.ds(starts[p], PARTS[p])
+        return pltpu.make_async_remote_copy(
+            src_ref=window.at[span, 1, rows], dst_ref=window.at[span, offsets, rows],
+            send_sem=piece_send.at[p, step], recv_sem=piece_recv.at[p],
+            device_id=(row + 2 * lane_to + core, g), device_id_type=MESH,
+        )
+
+    def across(p, hop):
+        rows = pl.ds(pl.multiple_of(lane * piece, piece), piece)
+        span = pl.ds(starts[p], PARTS[p])
+        return pltpu.make_async_remote_copy(
+            src_ref=window.at[span, held, rows], dst_ref=window.at[span, 2 * (1 - core), rows],
+            send_sem=across_send.at[p, hop], recv_sem=across_recv.at[p],
+            device_id=(goal, jnp.where(g == 0, half + hop, half - 1 - hop)), device_id_type=MESH,
+        )
+
+    def from_across(p):
+        span = pl.ds(starts[p], PARTS[p])
+        return pltpu.make_async_remote_copy(
+            src_ref=window.at[span, 1], dst_ref=window.at[span, 2 * core],
+            send_sem=across_send.at[p, 0], recv_sem=across_recv.at[p],
+            device_id=(goal, g), device_id_type=MESH,
+        )
 
     def block(p, owner):
         span = pl.ds(starts[p], PARTS[p])
@@ -100,7 +127,12 @@
 
     @pl.when(edge)
     def _():
-        greet(jnp.where(low, before, after), jnp.where(g < half, groups - 1, 0))
+        for q in range(LANES):
+            greet(feeders + 2 * q, jnp.where(g < half, groups - 1, 0))
+
+    @pl.when(forwards)
+    def _():
+        greet(row + core * (ROW - 1), g)
 
     for k in range(chunks):
         own_chunk(k).start()
@@ -109,24 +141,29 @@
     tiles[:, slots] = jnp.zeros((offsets, tile_rows, panels), tiles.dtype)
 
     pl.semaphore_wait(
-        barrier, groups - 1 + jnp.where(edge, 1, 2) + jnp.where(source, half, 0)
+        barrier, groups - 1 + jnp.where(edge, 1, 2) + jnp.where(end, half, 0) + jnp.where(splits, LANES - 1, 0)
     )
 
-    for k in range(chunks):
-        own_chunk(k).wait()
-
-        @pl.when(source)
-        def _():
-            for group in range(half, groups):
-                across(k, group).start()
-
-        @pl.when(jnp.logical_not(low))
-        def _():
-            to_before(k).start()
-
-        @pl.when(jnp.logical_not(high))
-        def _():
-            to_after(k).start()
+    for p, count in enumerate(PARTS):
+        for k in range(starts[p], starts[p] + count):
+            own_chunk(k).wait()
+
+        @pl.when(splits)
+        def _():
+            for step in range(1, LANES):
+                spread(p, step).start()
+            for hop in range(half):
+                across(p, hop).start()
+
+        for k in range(starts[p], starts[p] + count):
+
+            @pl.when(jnp.logical_not(low))
+            def _():
+                to_before(k).start()
+
+            @pl.when(jnp.logical_not(high))
+            def _():
+                to_after(k).start()
 
     tiles_in.wait()
     for offset in range(offsets):
@@ -143,9 +180,15 @@
     bands = groups // per_band
 
     def sample(k, sent):
-        to_after(k).wait_recv()
-        to_before(k).wait_recv()
-        panels_in = window[k].reshape(offsets * panels, WIDTH)
+        @pl.when(jnp.logical_not(low))
+        def _():
+            to_after(k).wait_recv()
+
+        @pl.when(jnp.logical_not(high))
+        def _():
+            to_before(k).wait_recv()
+
+        panels_in = window[k, 0:offsets].reshape(offsets * panels, WIDTH)
 
         def band(step, _):
             at = lax.rem(step + jnp.where(g < half, bands // 2, 0), bands)
@@ -171,6 +214,17 @@
         return 0
 
     for p, count in enumerate(PARTS):
+
+        @pl.when(forwards)
+        def _():
+            spread(p, 0).wait_recv()
+            for hop in range(half):
+                across(p, hop).start()
+
+        @pl.when(edge)
+        def _():
+            from_across(p).wait_recv()
+
         if count == 1:
             sample(starts[p], p)
             continue
@@ -212,12 +266,19 @@
 
     lax.fori_loop(1, groups, drain_block, 0)
 
+    for p in range(len(PARTS)):
+
+        @pl.when(splits)
+        def _():
+            for step in range(1, LANES):
+                spread(p, step).wait_send()
+
+        @pl.when(end)
+        def _():
+            for hop in range(half):
+                across(p, hop).wait_send()
+
     def drain(k, _):
-        @pl.when(source)
-        def _():
-            for group in range(half, groups):
-                across(k, group).wait_send()
-
         @pl.when(jnp.logical_not(low))
         def _():
             to_before(k).wait_send()
@@ -242,7 +303,7 @@
         kept = jnp.bfloat16
         coefficients = pl.pallas_call(
             functools.partial(kernel, blks, groups),
-            out_shape=jax.ShapeDtypeStruct((rank, columns), jnp.float32),
+            out_shape=pltpu.VMEM((rank, columns), jnp.float32),
             in_specs=[
                 pl.BlockSpec(memory_space=pl.ANY),
                 pl.BlockSpec(memory_space=pl.ANY),
@@ -252,7 +313,7 @@
             ],
             out_specs=pl.BlockSpec(memory_space=pltpu.VMEM),
             scratch_shapes=[
-                pltpu.VMEM((chunks, offsets, panels, WIDTH), kept),
+                pltpu.VMEM((chunks, offsets + 1, panels, WIDTH), kept),
                 pltpu.VMEM((offsets, slots + 1, tile_rows, panels), kept),
                 pltpu.VMEM((groups * tile_rows, offsets * panels), kept),
                 pltpu.VMEM((chunks, groups, tile_rows, WIDTH), kept),
@@ -262,7 +323,10 @@
                 pltpu.SemaphoreType.DMA((chunks + 2,)),
                 pltpu.SemaphoreType.DMA((2, chunks)),
                 pltpu.SemaphoreType.DMA((2, chunks)),
-                pltpu.SemaphoreType.DMA((chunks, groups // 2)),
+                pltpu.SemaphoreType.DMA((len(PARTS), LANES)),
+                pltpu.SemaphoreType.DMA((len(PARTS),)),
+                pltpu.SemaphoreType.DMA((len(PARTS), groups // 2)),
+                pltpu.SemaphoreType.DMA((len(PARTS),)),
                 pltpu.SemaphoreType.DMA((len(PARTS), groups)),
                 pltpu.SemaphoreType.DMA((len(PARTS), groups)),
             ],

time: 91.4 us -> 85.1 us (0.931)
  Pallas kernels: 88.2 us -> 82.7 us
  local copies, waits for them, and re-layouts: 2.06 us -> 0.88 us
    pallas_call x1, Pallas kernels: 88.2 us -> 82.7 us  [body(): pl.pallas_call(functools.partial(kernel, blks, groups), out_shape=pltpu.V...]
    unnamed x1, local copies, waits for them, and re-layouts: 2.06 us -> 0.88 us
where the time goes in v3:
time: 85.1 us; the launch traced here: 83.6 us
  Pallas kernels  82.7 us (97%)
  local copies, waits for them, and re-layouts  0.88 us (1%)
    pallas_call x1, Pallas kernels, body(): pl.pallas_call(functools.partial(kernel, blks, groups), out_shape=pltpu.V...  82.7 us

profile of v3, /device:TPU:504, one launch (start us, length us, event | category | flops | bytes accessed | tf_op | source)
XLA Modules:
  0.0 83.6 jit_solution(7512472486555634840)
XLA Ops:
  0.0 82.7 %shard_map.55 = f32[256,768]{1,0:T(8,128)S(1)} custom-call(bf16[512,768]{1,0:T(8,128)(2,1)} %sketch.1, bf16[1,1,3,6,128,512]{5,4,3,2,1,0:T(8,128)(2,1)} %far_tiles.1, s32[1,3,1,6]{3,2,1,0:T(1,128)} %bitcast.3, s32[1,1,8]{2,1,0:T(1,128)} %owner_route.1, bf16[1,1,1024,256]{3,2,1,0:T(8,128)(2,1)} %cluster_basis.1), custom_call_target="tpu_custom_call" | custom-call | tf_op jit(solution)/shard_map/pallas_call | solution.py:304
  82.7 0.9 %copy.7 = f32[1,1,256,768]{3,2,1,0:T(8,128)} copy(f32[1,1,256,768]{3,2,1,0:T(8,128)S(1)} %bitcast.2) | data formatting | bytes 1572864

commit v4 on v3

--- a/solution.py
+++ b/solution.py
@@ -109,13 +109,13 @@
             device_id=(b, peer), device_id_type=MESH,
         )
 
+    for k in range(chunks):
+        own_chunk(k).start()
+    tiles_in.start()
     barrier = pltpu.get_barrier_semaphore()
 
     def greet(blk, group):
         pl.semaphore_signal(barrier, inc=1, device_id=(blk, group), device_id_type=MESH)
-
-    for step in range(1, groups):
-        greet(b, lax.rem(g + step, groups))
 
     @pl.when(jnp.logical_not(low))
     def _():
@@ -134,9 +134,9 @@
     def _():
         greet(row + core * (ROW - 1), g)
 
-    for k in range(chunks):
-        own_chunk(k).start()
-    tiles_in.start()
+    for step in range(1, groups):
+        greet(b, lax.rem(g + step, groups))
+
     basis_in.start()
     tiles[:, slots] = jnp.zeros((offsets, tile_rows, panels), tiles.dtype)
 
@@ -240,24 +240,50 @@
     basis_t[...] = basis[...].T
     out[...] = jnp.zeros_like(out)
 
-    def gather(step, _):
-        near = step < half
-        peer = jnp.where(g < half, 0, half) + lax.rem(g + step, half)
-        peer = jnp.where(near, peer, lax.rem(peer + half, groups))
-
-        @pl.when(step > 0)
-        def _():
-            for p in range(len(PARTS)):
+    for p in range(len(PARTS)):
+
+        @pl.when(splits)
+        def _():
+            for step in range(1, LANES):
+                spread(p, step).wait_send()
+
+        @pl.when(end)
+        def _():
+            for hop in range(half):
+                across(p, hop).wait_send()
+
+    def drain(k, _):
+        @pl.when(jnp.logical_not(low))
+        def _():
+            to_before(k).wait_send()
+
+        @pl.when(jnp.logical_not(high))
+        def _():
+            to_after(k).wait_send()
+
+        return 0
+
+    lax.fori_loop(0, chunks, drain, 0)
+
+    for p, count in enumerate(PARTS):
+
+        def gather(step, _):
+            near = step < half
+            peer = jnp.where(g < half, 0, half) + lax.rem(g + step, half)
+            peer = jnp.where(near, peer, lax.rem(peer + half, groups))
+
+            @pl.when(step > 0)
+            def _():
                 from_peer(p, peer).wait_recv()
 
-        part = basis_t[:, pl.ds(pl.multiple_of(peer * tile_rows, tile_rows), tile_rows)]
-        for k in range(chunks):
-            out[:, k * WIDTH : (k + 1) * WIDTH] += jnp.dot(
-                part, received[k, peer], preferred_element_type=jnp.float32
-            )
-        return 0
-
-    lax.fori_loop(0, groups, gather, 0)
+            part = basis_t[:, pl.ds(pl.multiple_of(peer * tile_rows, tile_rows), tile_rows)]
+            for k in range(starts[p], starts[p] + count):
+                out[:, k * WIDTH : (k + 1) * WIDTH] += jnp.dot(
+                    part, received[k, peer], preferred_element_type=jnp.float32
+                )
+            return 0
+
+        lax.fori_loop(0, groups, gather, 0)
 
     def drain_block(step, _):
         for p in range(len(PARTS)):
@@ -265,31 +291,6 @@
         return 0
 
     lax.fori_loop(1, groups, drain_block, 0)
-
-    for p in range(len(PARTS)):
-
-        @pl.when(splits)
-        def _():
-            for step in range(1, LANES):
-                spread(p, step).wait_send()
-
-        @pl.when(end)
-        def _():
-            for hop in range(half):
-                across(p, hop).wait_send()
-
-    def drain(k, _):
-        @pl.when(jnp.logical_not(low))
-        def _():
-            to_before(k).wait_send()
-
-        @pl.when(jnp.logical_not(high))
-        def _():
-            to_after(k).wait_send()
-
-        return 0
-
-    lax.fori_loop(0, chunks, drain, 0)
 
 
 def solution(mesh):

time: 85.1 us -> 84.9 us (level)
  no operation moved by 1% of the time
where the time goes in v4:
time: 84.9 us; the launch traced here: 83.5 us
  Pallas kernels  82.6 us (97%)
  local copies, waits for them, and re-layouts  0.88 us (1%)
    pallas_call x1, Pallas kernels, body(): pl.pallas_call(functools.partial(kernel, blks, groups), out_shape=pltpu.V...  82.6 us

profile of v4, /device:TPU:504, one launch (start us, length us, event | category | flops | bytes accessed | tf_op | source)
XLA Modules:
  0.0 83.5 jit_solution(3391474161011923808)
XLA Ops:
  0.0 82.6 %shard_map.55 = f32[256,768]{1,0:T(8,128)S(1)} custom-call(bf16[512,768]{1,0:T(8,128)(2,1)} %sketch.1, bf16[1,1,3,6,128,512]{5,4,3,2,1,0:T(8,128)(2,1)} %far_tiles.1, s32[1,3,1,6]{3,2,1,0:T(1,128)} %bitcast.3, s32[1,1,8]{2,1,0:T(1,128)} %owner_route.1, bf16[1,1,1024,256]{3,2,1,0:T(8,128)(2,1)} %cluster_basis.1), custom_call_target="tpu_custom_call" | custom-call | tf_op jit(solution)/shard_map/pallas_call | solution.py:305
  82.6 0.9 %copy.7 = f32[1,1,256,768]{3,2,1,0:T(8,128)} copy(f32[1,1,256,768]{3,2,1,0:T(8,128)S(1)} %bitcast.2) | data formatting | bytes 1572864

commit v5 on v4

--- a/solution.py
+++ b/solution.py
@@ -20,7 +20,7 @@
     sketch, far_tiles, row_blocks, owner_route, cluster_basis, out,
     window, tiles, lefts, ordered, received, basis, basis_t,
     in_sem, halo_send, halo_recv, piece_send, piece_recv, across_send, across_recv,
-    block_send, block_recv,
+    block_send, block_recv, present,
 ):
     b = lax.axis_index("blk")
     g = lax.axis_index("group")
@@ -40,6 +40,14 @@
     goal = jnp.where(core == 0, lax.rem(row + blks - 1, blks), lax.rem(row + ROW, blks))
     feeders = jnp.where(low, lax.rem(row + blks - ROW, blks), lax.rem(row + ROW, blks)) + 1 - core
 
+    flip = lax.rem(row // ROW, 2) == 1
+    rank = jnp.where(flip, jnp.where(g < half, g + half, groups - 1 - g), g)
+
+    def at_rank(r):
+        return jnp.where(flip, jnp.where(r < half, groups - 1 - r, r - half), r)
+
+    together = (lane == 0) | (lane == LANES - 1)
+
     starts = [sum(PARTS[:p]) for p in range(len(PARTS))]
 
     def own_chunk(k):
@@ -82,7 +90,7 @@
         return pltpu.make_async_remote_copy(
             src_ref=window.at[span, held, rows], dst_ref=window.at[span, 2 * (1 - core), rows],
             send_sem=across_send.at[p, hop], recv_sem=across_recv.at[p],
-            device_id=(goal, jnp.where(g == 0, half + hop, half - 1 - hop)), device_id_type=MESH,
+            device_id=(goal, jnp.where(g == 0, groups - 1 - hop, hop)), device_id_type=MESH,
         )
 
     def from_across(p):
@@ -134,15 +142,26 @@
     def _():
         greet(row + core * (ROW - 1), g)
 
-    for step in range(1, groups):
-        greet(b, lax.rem(g + step, groups))
+    for r in range(groups):
+
+        @pl.when((r > rank) | (together & (r < rank)))
+        def _():
+            greet(b, at_rank(r))
 
     basis_in.start()
     tiles[:, slots] = jnp.zeros((offsets, tile_rows, panels), tiles.dtype)
 
     pl.semaphore_wait(
-        barrier, groups - 1 + jnp.where(edge, 1, 2) + jnp.where(end, half, 0) + jnp.where(splits, LANES - 1, 0)
+        barrier, jnp.where(together, groups - 1, rank) + jnp.where(edge, 1, 2) + jnp.where(end, half, 0) + jnp.where(splits, LANES - 1, 0)
     )
+
+    for r in range(groups - 1):
+
+        @pl.when((r < rank) & jnp.logical_not(together))
+        def _():
+            pl.semaphore_signal(
+                present.at[g], inc=1, device_id=(b, at_rank(r)), device_id_type=MESH
+            )
 
     for p, count in enumerate(PARTS):
         for k in range(starts[p], starts[p] + count):
@@ -190,6 +209,32 @@
 
         panels_in = window[k, 0:offsets].reshape(offsets * panels, WIDTH)
 
+        if sent is not None:
+
+            def one(r, _):
+                owner = jnp.where(
+                    together, lax.rem(r + jnp.where(g < half, half, 0), groups), at_rank(r)
+                )
+                ordered[k, owner] = jnp.dot(
+                    lefts[pl.ds(pl.multiple_of(owner * tile_rows, tile_rows), tile_rows), :],
+                    panels_in,
+                    preferred_element_type=jnp.float32,
+                ).astype(jnp.bfloat16)
+
+                @pl.when((r > rank) & jnp.logical_not(together))
+                def _():
+                    pl.semaphore_wait(present.at[owner], 1)
+
+                @pl.when(owner != g)
+                def _():
+                    block(sent, owner).start()
+
+                return 0
+
+            lax.fori_loop(0, groups, one, 0)
+            received[k, g] = ordered[k, g]
+            return 0
+
         def band(step, _):
             at = lax.rem(step + jnp.where(g < half, bands // 2, 0), bands)
             rows = jnp.dot(
@@ -200,12 +245,6 @@
             for part in range(per_band):
                 owner = at * per_band + part
                 ordered[k, owner] = rows[part * tile_rows : (part + 1) * tile_rows]
-                if sent is not None:
-
-                    @pl.when(owner != g)
-                    def _():
-                        block(sent, owner).start()
-
             return 0
 
         lax.fori_loop(0, bands, band, 0)
@@ -330,6 +369,7 @@
                 pltpu.SemaphoreType.DMA((len(PARTS),)),
                 pltpu.SemaphoreType.DMA((len(PARTS), groups)),
                 pltpu.SemaphoreType.DMA((len(PARTS), groups)),
+                pltpu.SemaphoreType.REGULAR((groups,)),
             ],
             compiler_params=pltpu.CompilerParams(
                 collective_id=0, has_side_effects=True, vmem_limit_bytes=60 * 1024 * 1024

time: 84.9 us -> 84.3 us (level); the launches traced: 83.5 us -> 84.1 us
  no operation moved by 1% of the time
where the time goes in v5:
time: 84.3 us; the launch traced here: 84.1 us
  Pallas kernels  83.2 us (99%)
  local copies, waits for them, and re-layouts  0.88 us (1%)
    pallas_call x1, Pallas kernels, body(): pl.pallas_call(functools.partial(kernel, blks, groups), out_shape=pltpu.V...  83.2 us

profile of v5, /device:TPU:504, one launch (start us, length us, event | category | flops | bytes accessed | tf_op | source)
XLA Modules:
  0.0 84.1 jit_solution(5748423441489814051)
XLA Ops:
  0.0 83.2 %shard_map.55 = f32[256,768]{1,0:T(8,128)S(1)} custom-call(bf16[512,768]{1,0:T(8,128)(2,1)} %sketch.1, bf16[1,1,3,6,128,512]{5,4,3,2,1,0:T(8,128)(2,1)} %far_tiles.1, s32[1,3,1,6]{3,2,1,0:T(1,128)} %bitcast.3, s32[1,1,8]{2,1,0:T(1,128)} %owner_route.1, bf16[1,1,1024,256]{3,2,1,0:T(8,128)(2,1)} %cluster_basis.1), custom_call_target="tpu_custom_call" | custom-call | tf_op jit(solution)/shard_map/pallas_call | solution.py:344
  83.3 0.9 %copy.7 = f32[1,1,256,768]{3,2,1,0:T(8,128)} copy(f32[1,1,256,768]{3,2,1,0:T(8,128)S(1)} %bitcast.2) | data formatting | bytes 1572864

commit v6 on v5

--- a/solution.py
+++ b/solution.py
@@ -252,13 +252,15 @@
 
         return 0
 
-    for p, count in enumerate(PARTS):
+    for p in range(len(PARTS)):
 
         @pl.when(forwards)
         def _():
             spread(p, 0).wait_recv()
             for hop in range(half):
                 across(p, hop).start()
+
+    for p, count in enumerate(PARTS):
 
         @pl.when(edge)
         def _():

time: 84.3 us -> 84.2 us (level)
  no operation moved by 1% of the time
where the time goes in v6:
time: 84.2 us; the launch traced here: 83.8 us
  Pallas kernels  82.9 us (98%)
  local copies, waits for them, and re-layouts  0.88 us (1%)
    pallas_call x1, Pallas kernels, body(): pl.pallas_call(functools.partial(kernel, blks, groups), out_shape=pltpu.V...  82.9 us

profile of v6, /device:TPU:504, one launch (start us, length us, event | category | flops | bytes accessed | tf_op | source)
XLA Modules:
  0.0 83.8 jit_solution(5970494891565845245)
XLA Ops:
  0.0 82.9 %shard_map.55 = f32[256,768]{1,0:T(8,128)S(1)} custom-call(bf16[512,768]{1,0:T(8,128)(2,1)} %sketch.1, bf16[1,1,3,6,128,512]{5,4,3,2,1,0:T(8,128)(2,1)} %far_tiles.1, s32[1,3,1,6]{3,2,1,0:T(1,128)} %bitcast.3, s32[1,1,8]{2,1,0:T(1,128)} %owner_route.1, bf16[1,1,1024,256]{3,2,1,0:T(8,128)(2,1)} %cluster_basis.1), custom_call_target="tpu_custom_call" | custom-call | tf_op jit(solution)/shard_map/pallas_call | solution.py:346
  82.9 0.9 %copy.7 = f32[1,1,256,768]{3,2,1,0:T(8,128)} copy(f32[1,1,256,768]{3,2,1,0:T(8,128)S(1)} %bitcast.2) | data formatting | bytes 1572864

commit v7 on v5

--- a/solution.py
+++ b/solution.py
@@ -46,7 +46,7 @@
     def at_rank(r):
         return jnp.where(flip, jnp.where(r < half, groups - 1 - r, r - half), r)
 
-    together = (lane == 0) | (lane == LANES - 1)
+    together = lane == LANES - 1
 
     starts = [sum(PARTS[:p]) for p in range(len(PARTS))]
 

time: 84.3 us -> 84.3 us (level)
  no operation moved by 1% of the time
where the time goes in v7:
time: 84.3 us; the launch traced here: 84.1 us
  Pallas kernels  83.2 us (99%)
  local copies, waits for them, and re-layouts  0.88 us (1%)
    pallas_call x1, Pallas kernels, body(): pl.pallas_call(functools.partial(kernel, blks, groups), out_shape=pltpu.V...  83.2 us

profile of v7, /device:TPU:504, one launch (start us, length us, event | category | flops | bytes accessed | tf_op | source)
XLA Modules:
  0.0 84.1 jit_solution(9865079972954833394)
XLA Ops:
  0.0 83.2 %shard_map.55 = f32[256,768]{1,0:T(8,128)S(1)} custom-call(bf16[512,768]{1,0:T(8,128)(2,1)} %sketch.1, bf16[1,1,3,6,128,512]{5,4,3,2,1,0:T(8,128)(2,1)} %far_tiles.1, s32[1,3,1,6]{3,2,1,0:T(1,128)} %bitcast.3, s32[1,1,8]{2,1,0:T(1,128)} %owner_route.1, bf16[1,1,1024,256]{3,2,1,0:T(8,128)(2,1)} %cluster_basis.1), custom_call_target="tpu_custom_call" | custom-call | tf_op jit(solution)/shard_map/pallas_call | solution.py:344
  83.2 0.9 %copy.7 = f32[1,1,256,768]{3,2,1,0:T(8,128)} copy(f32[1,1,256,768]{3,2,1,0:T(8,128)S(1)} %bitcast.2) | data formatting | bytes 1572864
